TPU v7x, 32 devices: a whole 2x2x4 slice. The times are simulated.
32 devices in a mesh: freq: 4 (over x, core), rcv: 8 (over z, y).
Axes of the slice: x: 2, y: 2, z: 4, core: 2. Of those that a mesh axis runs over, the one named last changes fastest.
Arguments:
- reflection: bfloat16 [8, 2, 2560, 2560], P('freq', None, 'rcv'), may hold values from -5 to 5, as said below
- starts: int32 [2560, 192], P('rcv'), may hold values from 8 to 56
- focusing: float32 [8, 2560, 2, 192], P('freq', 'rcv'), may hold values from -6 to 6
- residual: float32 [8, 2560, 2, 192], P('freq', 'rcv'), may hold values from -6 to 6
- direction: float32 [8, 2560, 2, 192], P('freq', 'rcv'), may hold values from -6 to 6
- gradient: float32 [8, 2560, 2, 192], P('freq', 'rcv'), may hold values from -30 to 30
Outputs:
- new_focusing: float32 [8, 2560, 2, 192], P('freq', 'rcv')
- new_residual: float32 [8, 2560, 2, 192], P('freq', 'rcv')
- new_direction: float32 [8, 2560, 2, 192], P('freq', 'rcv')
- green_field: float32 [8, 2560, 2, 192], P('freq', 'rcv')
- focal_correlation: float32 [8, 2, 192], P('freq')
Inputs may be any that keep to these rules, and one draw needn't show every extreme that they name: Each frequency's matrix is symmetric in source and receiver: reflection[f, c, s, r] = reflection[f, c, r, s].
All inputs are finite; a program needn't handle non-finite values.
Results may differ from a plain program's by a relative error of at most 0.0003.
The roundings to bfloat16 on the way count: a program that leaves them out, or rounds other values in their place, can miss the bound.
Values may be sent and summed in bfloat16 or wider, within the bound.
No kernel may reach another device: no remote copies, remote signals or barrier semaphores. Data moves between devices by JAX's collectives and lax.ppermute only.
A program may use at most 64 MiB of HBM per device.

v0:
```python
import math
import jax
import jax.numpy as jnp
from jax import lax
from jax.sharding import PartitionSpec as P

N = 2560
F = 8
TS = 64
band_start = 5
tiny = 1e-06
highest = lax.Precision.HIGHEST


def tables(count):
    times = jnp.arange(TS, dtype=jnp.float32)[:, None]
    bins = (jnp.arange(count, dtype=jnp.int32) + band_start).astype(jnp.float32)[None, :]
    phase = 2.0 * jnp.pi * times * bins / TS
    return (jnp.cos(phase), jnp.sin(phase))


def contract_time(table, values):
    return jnp.einsum("tf,frk->trk", table, values, precision=highest)


def contract_back(table, values):
    return jnp.einsum("tf,trk->frk", table, values, precision=highest)


def time_gate(field, forward_cos, forward_sin, back_cos, back_sin, limits, complement):
    real_part = field[:, :, 0]
    imag_part = field[:, :, 1]
    time_real = contract_time(forward_cos, real_part) - contract_time(forward_sin, imag_part)
    time_imag = contract_time(forward_sin, real_part) + contract_time(forward_cos, imag_part)
    clock = jnp.arange(TS, dtype=jnp.int32)[:, None, None]
    window = (clock < limits[None]).astype(jnp.float32)
    if complement:
        window = 1.0 - window
    kept_real = window * time_real
    kept_imag = window * time_imag
    out_real = (contract_back(back_cos, kept_real) + contract_back(back_sin, kept_imag)) / TS
    out_imag = (contract_back(back_cos, kept_imag) - contract_back(back_sin, kept_real)) / TS
    return jnp.stack([out_real, out_imag], axis=2)


def combine(total, conjugate):
    if conjugate:
        out_real = total[:, 0, :, 0] + total[:, 1, :, 1]
        out_imag = total[:, 0, :, 1] - total[:, 1, :, 0]
    else:
        out_real = total[:, 0, :, 0] - total[:, 1, :, 1]
        out_imag = total[:, 0, :, 1] + total[:, 1, :, 0]
    return jnp.stack([out_real, out_imag], axis=2)


def per_device(reflection, starts, focusing, residual, direction, gradient):
    local_rows = reflection.shape[2]
    groups = lax.axis_size("freq")
    position = lax.axis_index("freq")
    cos_table, sin_table = tables(F)

    def gate(field, complement):
        spread = lax.all_to_all(field, "freq", split_axis=1, concat_axis=0, tiled=True)
        share = local_rows // groups
        limits = lax.dynamic_slice_in_dim(starts, position * share, share, 0)
        gated_part = time_gate(
            spread, cos_table, sin_table, cos_table, sin_table, limits, complement
        )
        return lax.all_to_all(gated_part, "freq", split_axis=0, concat_axis=1, tiled=True)

    def accumulate(piece):
        return jnp.einsum("fpnm,fmqk->fpnqk", reflection, piece, preferred_element_type=jnp.float32)

    direction_low = direction.astype(jnp.bfloat16)
    focusing_low = focusing.astype(jnp.bfloat16)
    aimed_total = accumulate(lax.all_gather(direction_low, "rcv", axis=1, tiled=True))
    direction_image = combine(aimed_total, False)
    gamma = lax.psum(jnp.sum(gradient * gradient), ("freq", "rcv"))
    image = gate(direction_image, False)
    curvature = lax.psum(jnp.sum(image * image), ("freq", "rcv"))
    alpha = gamma / (curvature + tiny)
    new_focusing = focusing + alpha * direction
    new_residual = residual - alpha * image
    gated = gate(new_residual, False).astype(jnp.bfloat16)
    total = accumulate(lax.all_gather(gated, "rcv", axis=1, tiled=True))
    new_gradient = combine(total, True)
    new_gamma = lax.psum(jnp.sum(new_gradient * new_gradient), ("freq", "rcv"))
    new_direction = new_gradient + new_gamma / (gamma + tiny) * direction
    focus_total = accumulate(lax.all_gather(focusing_low, "rcv", axis=1, tiled=True))
    focusing_image = combine(focus_total, False)
    green_field = gate(focusing_image + alpha * direction_image, True)
    corr_real = jnp.sum(
        green_field[:, :, 0] * new_focusing[:, :, 0] + green_field[:, :, 1] * new_focusing[:, :, 1],
        axis=1,
    )
    corr_imag = jnp.sum(
        green_field[:, :, 1] * new_focusing[:, :, 0] - green_field[:, :, 0] * new_focusing[:, :, 1],
        axis=1,
    )
    partial_corr = jnp.stack([corr_real, corr_imag], axis=1)
    focal_correlation = lax.psum(partial_corr, "rcv") / math.sqrt(N)
    return (new_focusing, new_residual, new_direction, green_field, focal_correlation)


def solution(mesh):
    return jax.shard_map(
        per_device,
        mesh=mesh,
        in_specs=(
            P("freq", None, "rcv", None),
            P("rcv", None),
            P("freq", "rcv", None, None),
            P("freq", "rcv", None, None),
            P("freq", "rcv", None, None),
            P("freq", "rcv", None, None),
        ),
        out_specs=(
            P("freq", "rcv", None, None),
            P("freq", "rcv", None, None),
            P("freq", "rcv", None, None),
            P("freq", "rcv", None, None),
            P("freq", None, None),
        ),
        check_vma=False,
    )
```

profile of v0, /device:TPU:0, one launch (start us, length us, event | category | flops | bytes accessed | tf_op | source)
XLA Modules:
  0.0 475.7 jit_solution(8466674727431938095)
XLA Ops:
  10.4 89.0 %all-gather.4.cloned.1.call-done = bf16[2,2560,2,192]{3,2,0,1:T(2,128)(2,1)} async-done(((bf16[2,320,2,192]{3,2,0,1:T(2,128)(2,1)}), bf16[2,2560,2,192]{3,2,0,1:T(2,128)(2,1)}) %all-gather.4.cloned.1.call-update) | async-done | bytes 3932176 | tf_op jit(solution)/shard_map/all_gather | solution.py:76
  99.4 8.1 %fusion.2 = f32[2,2,320,2,192]{2,4,3,1,0:T(8,128)S(1)} fusion(bf16[2,2,320,2560]{3,2,1,0:T(8,128)(2,1)} %param.6, bf16[2,2560,2,192,1]{3,2,0,1,4:T(2,128)(2,1)} %bitcast.192), kind=kOutput, calls=%fused_computation.2 | convolution fusion | flops 2516582400 | bytes 12451840 | tf_op jit(solution)/shard_map/fpnm,fmqk->fpnqk/dot_general | solution.py:72
  107.7 2.0 copy.107
  109.7 3.5 all-to-all-start
  114.6 2.2 copy.125
  117.2 13.3 %all-to-all-done = f32[2,320,2,192]{3,0,2,1:T(2,128)S(1)} async-done(((f32[2,320,2,192]{3,0,2,1:T(2,128)}), f32[2,320,2,192]{3,0,2,1:T(2,128)S(1)}, u32[]{:S(2)}, u32[]{:S(2)}) %all-to-all-start) | async-done | bytes 983072 | tf_op jit(solution)/shard_map/all_to_all | solution.py:63
  132.6 4.4 fusion.27
  137.1 4.4 fusion.26
  141.5 5.0 %subtract_select_fusion.1 = f32[64,80,192]{2,0,1:T(8,128)S(1)} fusion(f32[64,80,192]{2,0,1:T(8,128)S(1)} %fusion.27, s32[80,192]{1,0:T(8,128)S(1)} %copy.102, f32[8,80,2,192]{3,0,1,2:T(8,128)S(1)} %all_to_all.69, f32[8]{0:T(128)S(1)} %add_convert_fusion, f32[64]{0:T(128)S(1)} %iota_multiply_fusion), kind=kOutput, calls=%fused_computation.15 | convolution fusion | flops 97321984 | bytes 9913344 | tf_op jit(solution)/shard_map/tf,frk->trk/dot_general | solution.py:23
  146.6 2.6 fusion.67
  149.2 4.9 %add_select_fusion.1 = f32[64,80,192]{2,0,1:T(8,128)S(1)} fusion(f32[64,80,192]{2,0,1:T(8,128)S(1)} %fusion.26, s32[80,192]{1,0:T(8,128)S(1)} %copy.102, f32[8,80,2,192]{3,0,1,2:T(8,128)S(1)} %all_to_all.69, f32[8]{0:T(128)S(1)} %add_convert_fusion, f32[64]{0:T(128)S(1)} %iota_multiply_fusion), kind=kOutput, calls=%fused_computation.14 | convolution fusion | flops 97321984 | bytes 9913344 | tf_op jit(solution)/shard_map/tf,frk->trk/dot_general | solution.py:23
  154.1 2.9 fusion.25
  156.9 2.6 fusion.64
  159.6 2.7 fusion.23
  163.8 3.5 all-to-all-start.1
  168.3 16.2 %all-to-all-done.1 = f32[8,80,2,192]{3,1,2,0:T(8,128)S(1)} async-done(((f32[8,80,2,192]{3,1,2,0:T(8,128)}), f32[8,80,2,192]{3,1,2,0:T(8,128)S(1)}, u32[]{:S(2)}, u32[]{:S(2)}) %all-to-all-start.1) | async-done | bytes 983072 | tf_op jit(solution)/shard_map/all_to_all | solution.py:69
  187.2 38.8 %all-reduce = (f32[]{:T(128)}, f32[]{:T(128)}) all-reduce(f32[]{:T(128)} %multiply_reduce_fusion.2, f32[]{:T(128)} %multiply_reduce_fusion), channel_id=1, replica_groups=mesh['freq'=4,'rcv'=8] {'freq','rcv'}, use_global_device_ids=true, to_apply=%region_1.0 | all-reduce | flops 2 | bytes 16 | tf_op jit(solution)/shard_map/psum | solution.py:78
  228.7 20.6 %all_to_all.90 = f32[2,320,2,192]{3,2,0,1:T(2,128)S(1)} all-to-all(f32[2,320,2,192]{3,2,0,1:T(2,128)S(1)} %copy.115), channel_id=1, replica_groups=mesh['freq'=4,'rcv'=8] {'freq'}, dimensions={1} | all-to-all | bytes 1966080 | tf_op jit(solution)/shard_map/all_to_all | solution.py:63
  249.6 2.1 copy.117
  251.7 2.6 all_to_all.74
  254.2 4.4 fusion.29
  258.7 4.4 fusion.28
  263.1 5.0 %subtract_select_fusion = f32[64,80,192]{2,0,1:T(8,128)S(1)} fusion(f32[64,80,192]{2,0,1:T(8,128)S(1)} %fusion.29, s32[80,192]{1,0:T(8,128)S(1)} %copy.102, f32[8,80,2,192]{3,0,1,2:T(8,128)S(1)} %all_to_all.74, f32[8]{0:T(128)S(1)} %add_convert_fusion, f32[64]{0:T(128)S(1)} %iota_multiply_fusion), kind=kOutput, calls=%fused_computation.13 | convolution fusion | flops 97321984 | bytes 9913344 | tf_op jit(solution)/shard_map/tf,frk->trk/dot_general | solution.py:23
  268.2 2.6 fusion.61
  270.8 4.9 %add_select_fusion = f32[64,80,192]{2,0,1:T(8,128)S(1)} fusion(f32[64,80,192]{2,0,1:T(8,128)S(1)} %fusion.28, s32[80,192]{1,0:T(8,128)S(1)} %copy.102, f32[8,80,2,192]{3,0,1,2:T(8,128)S(1)} %all_to_all.74, f32[8]{0:T(128)S(1)} %add_convert_fusion, f32[64]{0:T(128)S(1)} %iota_multiply_fusion), kind=kOutput, calls=%fused_computation.12 | convolution fusion | flops 97321984 | bytes 9913344 | tf_op jit(solution)/shard_map/tf,frk->trk/dot_general | solution.py:23
  275.7 2.6 fusion.21
  278.3 2.8 fusion.58
  281.1 2.6 fusion.19
  284.0 12.6 %all_to_all.91 = bf16[8,80,2,192]{3,1,2,0:T(8,128)(2,1)S(1)} all-to-all(bf16[8,80,2,192]{3,1,2,0:T(8,128)(2,1)S(1)} %copy.118), channel_id=1, replica_groups=mesh['freq'=4,'rcv'=8] {'freq'}, dimensions={0} | all-to-all | bytes 983040 | tf_op jit(solution)/shard_map/all_to_all | solution.py:69
  298.3 8.2 %fusion.4 = f32[2,2,320,2,192]{2,4,0,3,1:T(8,128)S(1)} fusion(bf16[2,2560,2,192,1]{3,2,0,1,4:T(2,128)(2,1)} %bitcast.190, bf16[2,2,320,2560]{3,2,1,0:T(8,128)(2,1)} %param.6), kind=kOutput, calls=%fused_computation.4 | convolution fusion | flops 2516582400 | bytes 12451840 | tf_op jit(solution)/shard_map/fpnm,fmqk->fpnqk/dot_general | solution.py:72
  307.8 2.6 copy.131
  310.4 19.7 %all_to_all.92 = f32[2,320,2,192]{3,0,2,1:T(2,128)S(1)} all-to-all(f32[2,320,2,192]{3,0,2,1:T(2,128)S(1)} %copy.131), channel_id=1, replica_groups=mesh['freq'=4,'rcv'=8] {'freq'}, dimensions={1} | all-to-all | bytes 1966080 | tf_op jit(solution)/shard_map/all_to_all | solution.py:63
  330.3 2.1 copy.133
  332.4 2.6 all_to_all.79
  335.0 4.4 fusion.31
  339.4 4.4 fusion.30
  343.8 5.4 %subtract_multiply_fusion = f32[64,80,192]{2,0,1:T(8,128)S(1)} fusion(f32[64,80,192]{2,0,1:T(8,128)S(1)} %fusion.31, s32[80,192]{1,0:T(8,128)S(1)} %copy.102, f32[8,80,2,192]{3,0,1,2:T(8,128)S(1)} %all_to_all.79, f32[8]{0:T(128)S(1)} %add_convert_fusion, f32[64]{0:T(128)S(1)} %iota_multiply_fusion), kind=kOutput, calls=%fused_computation.10 | convolution fusion | flops 99288064 | bytes 9913344 | tf_op jit(solution)/shard_map/tf,frk->trk/dot_general | solution.py:23
  349.3 2.6 fusion.55
  351.9 5.2 %add_multiply_fusion = f32[64,80,192]{2,0,1:T(8,128)S(1)} fusion(f32[64,80,192]{2,0,1:T(8,128)S(1)} %fusion.30, s32[80,192]{1,0:T(8,128)S(1)} %copy.102, f32[8,80,2,192]{3,0,1,2:T(8,128)S(1)} %all_to_all.79, f32[8]{0:T(128)S(1)} %add_convert_fusion, f32[64]{0:T(128)S(1)} %iota_multiply_fusion), kind=kOutput, calls=%fused_computation.9 | convolution fusion | flops 99288064 | bytes 9913344 | tf_op jit(solution)/shard_map/tf,frk->trk/dot_general | solution.py:23
  357.2 2.6 fusion.17
  359.8 2.8 fusion.52
  362.6 2.7 fusion.15
  366.9 3.5 all-to-all-start.5
  372.5 15.1 %all-to-all-done.5 = f32[8,80,2,192]{3,1,2,0:T(8,128)S(1)} async-done(((f32[8,80,2,192]{3,1,2,0:T(8,128)}), f32[8,80,2,192]{3,1,2,0:T(8,128)S(1)}, u32[]{:S(2)}, u32[]{:S(2)}) %all-to-all-start.5) | async-done | bytes 983072 | tf_op jit(solution)/shard_map/all_to_all | solution.py:69
  390.4 10.1 %fusion.9 = f32[2,2,320,2,192]{2,4,1,3,0:T(8,128)S(1)} fusion(bf16[2,2,320,2560]{3,2,1,0:T(8,128)(2,1)} %param.6, bf16[2,2560,2,192,1]{3,2,0,1,4:T(2,128)(2,1)} %bitcast.191), kind=kOutput, calls=%fused_computation.17 | convolution fusion | flops 2516582400 | bytes 12451840 | tf_op jit(solution)/shard_map/fpnm,fmqk->fpnqk/dot_general | solution.py:72
  402.7 39.1 %psum.30 = f32[]{:T(128)} all-reduce(f32[]{:T(128)} %multiply_reduce_fusion.1), channel_id=1, replica_groups=mesh['freq'=4,'rcv'=8] {'freq','rcv'}, use_global_device_ids=true, to_apply=%region_5.0 | all-reduce | flops 1 | bytes 8 | tf_op jit(solution)/shard_map/psum | solution.py:87
  442.5 2.5 multiply_add_fusion
  446.5 20.7 %psum.31 = f32[2,2,192]{2,0,1:T(2,128)S(1)} all-reduce(f32[2,2,192]{2,0,1:T(2,128)S(1)} %pad_maximum_fusion.5), channel_id=1, replica_groups=mesh['freq'=4,'rcv'=8] {'rcv'}, use_global_device_ids=true, to_apply=%region_8.0 | all-reduce | flops 768 | bytes 6144 | tf_op jit(solution)/shard_map/psum | solution.py:101
  (73 shorter events, 28.5 us)
Async XLA Ops:
  7.2 109.8 %copy-start = (s32[320,192]{0,1:T(8,128)S(1)}, s32[320,192]{0,1:T(8,128)}, u32[]{:S(2)}) copy-start(s32[320,192]{0,1:T(8,128)} %param.7) | copy-start | bytes 737284
  7.2 92.2 %all-gather.4.cloned.1.call-start = ((), (), s32[]{:S(2)}) async-start(), calls=%async_computation.6 | async-start | bytes 5898240 | tf_op jit(solution)/shard_map/all_gather | solution.py:76
  107.6 9.2 %copy-start.2 = (f32[2,320,1,192]{1,3,0,2:T(8,128)}, f32[2,320,1,192]{1,3,0,2:T(8,128)S(1)}, u32[]{:S(2)}) copy-start(f32[2,320,1,192]{1,3,0,2:T(8,128)S(1)} %fusion.39) | copy-start | bytes 1474564
  109.7 20.8 %all-to-all-start = ((f32[2,320,2,192]{3,0,2,1:T(2,128)}), f32[2,320,2,192]{3,0,2,1:T(2,128)S(1)}, u32[]{:S(2)}, u32[]{:S(2)}) async-start(f32[2,320,2,192]{3,0,2,1:T(2,128)} %copy.107), calls=%async_computation | async-start | bytes 2621440 | tf_op jit(solution)/shard_map/all_to_all | solution.py:63
  113.3 185.0 %all-gather.8.cloned.1.call-start = ((), (), s32[]{:S(2)}) async-start(), calls=%async_computation.8 | async-start | bytes 5898240 | tf_op jit(solution)/shard_map/all_gather | solution.py:89
  162.2 5.2 %copy-start.8 = (f32[2,320,2,192]{1,3,2,0:T(8,128)S(1)}, f32[2,320,2,192]{1,3,2,0:T(8,128)}, u32[]{:S(2)}) copy-start(f32[2,320,2,192]{1,3,2,0:T(8,128)} %param.11) | copy-start | bytes 2949124
  163.8 20.8 %all-to-all-start.1 = ((f32[8,80,2,192]{3,1,2,0:T(8,128)}), f32[8,80,2,192]{3,1,2,0:T(8,128)S(1)}, u32[]{:S(2)}, u32[]{:S(2)}) async-start(f32[8,80,2,192]{3,1,2,0:T(8,128)} %copy.110), calls=%async_computation.1 | async-start | bytes 2621440 | tf_op jit(solution)/shard_map/all_to_all | solution.py:69
  167.4 223.1 %all-gather.6.cloned.1.call-start = ((), (), s32[]{:S(2)}) async-start(), calls=%async_computation.7 | async-start | bytes 5898240 | tf_op jit(solution)/shard_map/all_gather | solution.py:85
  298.3 8.3 %copy-start.3 = (f32[2,320,1,192]{1,3,0,2:T(8,128)S(1)}, f32[2,320,1,192]{1,3,0,2:T(8,128)}, u32[]{:S(2)}) copy-start(f32[2,320,1,192]{1,3,0,2:T(8,128)} %copy-done.2) | copy-start | bytes 1474564
  366.9 20.8 %all-to-all-start.5 = ((f32[8,80,2,192]{3,1,2,0:T(8,128)}), f32[8,80,2,192]{3,1,2,0:T(8,128)S(1)}, u32[]{:S(2)}, u32[]{:S(2)}) async-start(f32[8,80,2,192]{3,1,2,0:T(8,128)} %copy.134), calls=%async_computation.5 | async-start | bytes 2621440 | tf_op jit(solution)/shard_map/all_to_all | solution.py:69
  400.6 41.9 %copy-start.4 = (f32[2,320,2,192]{1,3,2,0:T(8,128)S(1)}, f32[2,320,2,192]{1,3,2,0:T(8,128)}, u32[]{:S(2)}) copy-start(f32[2,320,2,192]{1,3,2,0:T(8,128)} %param.10) | copy-start | bytes 2949124
  402.7 43.4 %copy-start.6 = (f32[2,320,1,192]{1,3,0,2:T(8,128)S(1)}, f32[2,320,1,192]{1,3,0,2:T(8,128)}, u32[]{:S(2)}) copy-start(f32[2,320,1,192]{1,3,0,2:T(8,128)} %copy.160) | copy-start | bytes 1474564
  441.8 27.1 %copy-start.1 = (s32[320,192]{0,1:T(8,128)S(1)}, s32[320,192]{0,1:T(8,128)}, u32[]{:S(2)}) copy-start(s32[320,192]{0,1:T(8,128)} %param.7) | copy-start | bytes 737284
  442.5 3.6 copy-start.7
  445.1 22.7 %copy-start.5 = (f32[2,320,2,192]{1,3,0,2:T(8,128)S(1)}, f32[2,320,2,192]{1,3,0,2:T(8,128)}, u32[]{:S(2)}) copy-start(f32[2,320,2,192]{1,3,0,2:T(8,128)} %get-tuple-element.33) | copy-start | bytes 2949124
Sparse Core Ops, SparseCore 0:
  10.7 88.5 all-gather.3
  117.0 84.5 all-gather.7
  298.4 84.9 all-gather.5
where the time goes:
time: 480 us; the launch traced here: 476 us
  blocking collectives  151 us (31%)
  waiting for transfers between devices  134 us (28%)
  matrix products  116 us (24%)
  local copies, waits for them, and re-layouts  36.4 us (8%)
  between operations  17.1 us (4%)
  starting transfers between devices  10.7 us (2%)
  other arithmetic  10.5 us (2%)
    all_gather x1, waiting for transfers between devices, per_device(): lax.all_gather(direction_low, 'rcv', axis=1, tiled=True)  89 us
    dot_general x12, matrix products, contract_time(): return jnp.einsum('tf,frk->trk', table, values, precision=highest)  57 us
    all_to_all x2, blocking collectives, gate(): lax.all_to_all(field, 'freq', split_axis=1, concat_axis=0, tiled=True)  40.3 us
    psum x1, blocking collectives, per_device(): new_gamma = lax.psum(jnp.sum(new_gradient * new_gradient), ('freq', 'rcv'))  39.1 us
    psum x1, blocking collectives, per_device(): gamma = lax.psum(jnp.sum(gradient * gradient), ('freq', 'rcv'))  38.8 us
    dot_general x12, matrix products, contract_back(): return jnp.einsum('tf,trk->frk', table, values, precision=highest)  32.3 us
    all_to_all x2, waiting for transfers between devices, gate(): lax.all_to_all(gated_part, 'freq', split_axis=0, concat_axis=1, tiled=True)  31.3 us
    dot_general x3, matrix products, accumulate(): jnp.einsum('fpnm,fmqk->fpnqk', reflection, piece, preferred_element_type=...  26.4 us
  transfers between devices with their start and end apart: 6, of which 4 were waited for; matrix products, arithmetic and copies ran while one was open for 26% of the time, Pallas kernels for 0%

commit v1 on v0

--- a/solution.py
+++ b/solution.py
@@ -1,3 +1,4 @@
+import functools
 import math
 import jax
 import jax.numpy as jnp
@@ -10,6 +11,29 @@
 band_start = 5
 tiny = 1e-06
 highest = lax.Precision.HIGHEST
+
+
+def fit_the_sources_all(array_in, pos_dim, join_dim):
+    frame_out = lax.axis_size("freq")
+    opened = lax.axis_index("freq")
+    mixed_arr, high = (frame_out, opened)
+    w_next = array_in.shape[pos_dim] // mixed_arr
+    current_arr = list(array_in.shape)
+    current_arr[pos_dim] = w_next
+    y2 = current_arr[join_dim]
+    current_arr[join_dim] = y2 * mixed_arr
+    a_next = jnp.zeros(current_arr, array_in.dtype)
+    idx = 0
+    while idx < mixed_arr:
+        tmp = lax.dynamic_slice_in_dim(array_in, (high ^ idx) * w_next, w_next, axis=pos_dim)
+        if idx:
+            tmp = lax.ppermute(tmp, "freq", tuple(((m, m ^ idx) for m in range(mixed_arr))))
+        a_next = lax.dynamic_update_slice_in_dim(a_next, tmp, (high ^ idx) * y2, axis=join_dim)
+        idx += 1
+    return a_next
+
+
+_touch_bench = functools.partial(fit_the_sources_all, pos_dim=1, join_dim=0)
 
 
 def tables(count):
@@ -60,7 +84,7 @@
     cos_table, sin_table = tables(F)
 
     def gate(field, complement):
-        spread = lax.all_to_all(field, "freq", split_axis=1, concat_axis=0, tiled=True)
+        spread = _touch_bench(field)
         share = local_rows // groups
         limits = lax.dynamic_slice_in_dim(starts, position * share, share, 0)
         gated_part = time_gate(

time: 480 us -> 498 us (1.038)
  waiting for transfers between devices: 134 us -> 179 us
  blocking collectives: 151 us -> 112 us
    all_to_all x2 -> x0, blocking collectives: 40.3 us -> none  [gate(): lax.all_to_all(field, 'freq', split_axis=1, concat_axis=0, tiled=True)]
    ppermute x0 -> x9, waiting for transfers between devices: none -> 31 us  [fit_the_sources_all(): lax.ppermute(tmp, 'freq', tuple(((m, m ^ idx) for m in range(mixed_arr))))]
    all_gather x1, waiting for transfers between devices: 0.01 us -> 28.6 us  [per_device(): total = accumulate(lax.all_gather(gated, 'rcv', axis=1, tiled=True))]
    all_gather x1, waiting for transfers between devices: 0.02 us -> 19.8 us  [per_device(): lax.all_gather(focusing_low, 'rcv', axis=1, tiled=True)]
    all_to_all x2, waiting for transfers between devices: 31.3 us -> 14.4 us  [gate(): lax.all_to_all(gated_part, 'freq', split_axis=0, concat_axis=1, tiled=True)]
    all_to_all x1 -> x0, waiting for transfers between devices: 13.3 us -> none  [gate(): lax.all_to_all(field, 'freq', split_axis=1, concat_axis=0, tiled=True)]
    all_to_all x9 -> x0, local copies, waits for them, and re-layouts: 12 us -> none  [gate(): lax.all_to_all(field, 'freq', split_axis=1, concat_axis=0, tiled=True)]
    ppermute x0 -> x6, local copies, waits for them, and re-layouts: none -> 7.91 us  [fit_the_sources_all(): lax.ppermute(tmp, 'freq', tuple(((m, m ^ idx) for m in range(mixed_arr))))]
  transfers between devices with their start and end apart: 6 -> 14, of which waited for: 4 -> 10; matrix products, arithmetic and copies ran while one was open for 26% -> 22% of each run, Pallas kernels for 0% -> 0%
where the time goes in v1:
time: 498 us; the launch traced here: 493 us
  waiting for transfers between devices  179 us (36%)
  matrix products  117 us (23%)
  blocking collectives  112 us (22%)
  local copies, waits for them, and re-layouts  41.2 us (8%)
  between operations  17.2 us (3%)
  starting transfers between devices  13.7 us (3%)
  other arithmetic  13.5 us (3%)
    all_gather x1, waiting for transfers between devices, per_device(): lax.all_gather(direction_low, 'rcv', axis=1, tiled=True)  85.3 us
    dot_general x12, matrix products, contract_time(): return jnp.einsum('tf,frk->trk', table, values, precision=highest)  57.3 us
    psum x1, blocking collectives, per_device(): gamma = lax.psum(jnp.sum(gradient * gradient), ('freq', 'rcv'))  39 us
    psum x1, blocking collectives, per_device(): new_gamma = lax.psum(jnp.sum(new_gradient * new_gradient), ('freq', 'rcv'))  38.6 us
    dot_general x12, matrix products, contract_back(): return jnp.einsum('tf,trk->frk', table, values, precision=highest)  32.1 us
    ppermute x9, waiting for transfers between devices, fit_the_sources_all(): lax.ppermute(tmp, 'freq', tuple(((m, m ^ idx) for m in range(mixed_arr))))  31 us
    all_gather x1, waiting for transfers between devices, per_device(): total = accumulate(lax.all_gather(gated, 'rcv', axis=1, tiled=True))  28.6 us
    dot_general x3, matrix products, accumulate(): jnp.einsum('fpnm,fmqk->fpnqk', reflection, piece, preferred_element_type=...  27.3 us
  transfers between devices with their start and end apart: 14, of which 10 were waited for; matrix products, arithmetic and copies ran while one was open for 22% of the time, Pallas kernels for 0%

profile of v1, /device:TPU:0, one launch (start us, length us, event | category | flops | bytes accessed | tf_op | source)
XLA Modules:
  0.0 493.4 jit_solution(13444730835810371648)
XLA Ops:
  14.1 85.3 %all-gather.4.cloned.1.call-done = bf16[2,2560,2,192]{3,2,0,1:T(2,128)(2,1)} async-done(((bf16[2,320,2,192]{3,2,0,1:T(2,128)(2,1)}), bf16[2,2560,2,192]{3,2,0,1:T(2,128)(2,1)}) %all-gather.4.cloned.1.call-update) | async-done | bytes 3932176 | tf_op jit(solution)/shard_map/all_gather | solution.py:100
  99.4 8.1 %fusion.2 = f32[2,2,320,2,192]{2,4,3,1,0:T(8,128)S(1)} fusion(bf16[2,2,320,2560]{3,2,1,0:T(8,128)(2,1)} %param.6, bf16[2,2560,2,192,1]{3,2,0,1,4:T(2,128)(2,1)} %bitcast.173), kind=kOutput, calls=%fused_computation.2 | convolution fusion | flops 2516582400 | bytes 12451840 | tf_op jit(solution)/shard_map/fpnm,fmqk->fpnqk/dot_general | solution.py:96
  111.0 2.5 copy.124
  115.3 5.8 %collective-permute-done.1 = f32[2,80,2,192]{1,3,0,2:T(8,128)} collective-permute-done((f32[2,80,2,192]{1,3,0,2:T(8,128)S(1)}, f32[2,80,2,192]{1,3,0,2:T(8,128)}, u32[]{:S(2)}, u32[]{:S(2)}) %collective-permute-start.1) | collective-permute-done | bytes 245792 | tf_op jit(solution)/shard_map/ppermute | solution.py:30
  122.4 6.3 %collective-permute-done.2 = f32[2,80,2,192]{1,3,0,2:T(8,128)} collective-permute-done((f32[2,80,2,192]{1,3,0,2:T(8,128)}, f32[2,80,2,192]{1,3,0,2:T(8,128)}, u32[]{:S(2)}, u32[]{:S(2)}) %collective-permute-start.2) | collective-permute-done | bytes 245792 | tf_op jit(solution)/shard_map/ppermute | solution.py:30
  131.8 4.4 fusion.29
  136.2 4.4 fusion.28
  140.6 5.1 %subtract_select_fusion.1 = f32[64,80,192]{2,0,1:T(8,128)S(1)} fusion(f32[64,80,192]{2,0,1:T(8,128)S(1)} %fusion.29, s32[80,192]{1,0:T(8,128)S(1)} %copy.111, f32[8,80,2,192]{3,0,1,2:T(8,128)S(1)} %constant_dynamic-update-slice_fusion.7, f32[8]{0:T(128)S(1)} %add_convert_fusion, f32[64]{0:T(128)S(1)} %iota_multiply_fusion), kind=kOutput, calls=%fused_computation.15 | convolution fusion | flops 97321984 | bytes 9913344 | tf_op jit(solution)/shard_map/tf,frk->trk/dot_general | solution.py:47
  145.7 2.6 fusion.73
  148.3 4.9 add_select_fusion.1
  153.2 2.7 fusion.25
  155.9 2.8 fusion.70
  158.7 2.7 fusion.23
  162.9 3.5 all-to-all-start
  166.5 19.8 %all-gather.8.cloned.1.call-done = bf16[2,2560,2,192]{3,2,0,1:T(2,128)(2,1)} async-done(((bf16[2,320,2,192]{3,2,0,1:T(2,128)(2,1)}), bf16[2,2560,2,192]{3,2,0,1:T(2,128)(2,1)}) %all-gather.8.cloned.1.call-update) | async-done | bytes 3932176 | tf_op jit(solution)/shard_map/all_gather | solution.py:113
  186.2 9.1 %fusion.4 = f32[2,2,320,2,192]{2,4,0,3,1:T(8,128)} fusion(bf16[2,2560,2,192,1]{3,2,0,1,4:T(2,128)(2,1)} %bitcast.172, bf16[2,2,320,2560]{3,2,1,0:T(8,128)(2,1)} %param.6), kind=kOutput, calls=%fused_computation.4 | convolution fusion | flops 2516582400 | bytes 12451840 | tf_op jit(solution)/shard_map/fpnm,fmqk->fpnqk/dot_general | solution.py:96
  196.2 2.5 fusion.35
  198.8 39.0 %all-reduce = (f32[]{:T(128)}, f32[]{:T(128)}) all-reduce(f32[]{:T(128)} %multiply_reduce_fusion.2, f32[]{:T(128)} %multiply_reduce_fusion), channel_id=1, replica_groups=mesh['freq'=4,'rcv'=8] {'freq','rcv'}, use_global_device_ids=true, to_apply=%region_1.0 | all-reduce | flops 2 | bytes 16 | tf_op jit(solution)/shard_map/psum | solution.py:102
  242.1 2.3 collective-permute-start.7
  252.7 2.0 collective-permute-done.7
  256.2 6.5 %collective-permute-done.8 = f32[2,80,2,192]{1,3,0,2:T(8,128)} collective-permute-done((f32[2,80,2,192]{1,3,0,2:T(8,128)}, f32[2,80,2,192]{1,3,0,2:T(8,128)}, u32[]{:S(2)}, u32[]{:S(2)}) %collective-permute-start.8) | collective-permute-done | bytes 245792 | tf_op jit(solution)/shard_map/ppermute | solution.py:30
  265.1 5.1 %collective-permute-done.4 = f32[2,80,2,192]{3,0,1,2:T(2,128)} collective-permute-done((f32[2,80,2,192]{3,0,1,2:T(2,128)}, f32[2,80,2,192]{3,0,1,2:T(2,128)}, u32[]{:S(2)}, u32[]{:S(2)}) %collective-permute-start.4) | collective-permute-done | bytes 245792 | tf_op jit(solution)/shard_map/ppermute | solution.py:30
  271.4 5.3 %collective-permute-done.5 = f32[2,80,2,192]{3,0,1,2:T(2,128)} collective-permute-done((f32[2,80,2,192]{3,0,1,2:T(2,128)}, f32[2,80,2,192]{3,0,1,2:T(2,128)}, u32[]{:S(2)}, u32[]{:S(2)}) %collective-permute-start.5) | collective-permute-done | bytes 245792 | tf_op jit(solution)/shard_map/ppermute | solution.py:30
  278.1 4.4 fusion.31
  282.5 4.6 fusion.30
  287.2 4.9 subtract_select_fusion
  292.0 2.6 fusion.67
  294.7 5.1 %add_select_fusion = f32[64,80,192]{2,0,1:T(8,128)S(1)} fusion(f32[64,80,192]{2,0,1:T(8,128)S(1)} %fusion.30, s32[80,192]{1,0:T(8,128)S(1)} %copy.111, f32[8,80,2,192]{3,0,1,2:T(8,128)S(1)} %get-tuple-element.47, f32[8]{0:T(128)S(1)} %add_convert_fusion, f32[64]{0:T(128)S(1)} %iota_multiply_fusion), kind=kOutput, calls=%fused_computation.12 | convolution fusion | flops 97321984 | bytes 9913344 | tf_op jit(solution)/shard_map/tf,frk->trk/dot_general | solution.py:47
  299.8 2.6 fusion.64
  302.4 2.6 fusion.21
  305.0 2.6 fusion.19
  307.9 12.8 %all_to_all.36 = bf16[8,80,2,192]{3,1,2,0:T(8,128)(2,1)S(1)} all-to-all(bf16[8,80,2,192]{3,1,2,0:T(8,128)(2,1)S(1)} %copy.125), channel_id=1, replica_groups=mesh['freq'=4,'rcv'=8] {'freq'}, dimensions={0} | all-to-all | bytes 983040 | tf_op jit(solution)/shard_map/all_to_all | solution.py:93
  322.3 4.4 fusion.33
  326.7 4.4 fusion.32
  331.1 5.4 %subtract_multiply_fusion = f32[64,80,192]{2,0,1:T(8,128)S(1)} fusion(f32[64,80,192]{2,0,1:T(8,128)S(1)} %fusion.33, s32[80,192]{1,0:T(8,128)S(1)} %copy.111, f32[8,80,2,192]{3,0,1,2:T(8,128)S(1)} %get-tuple-element.48, f32[8]{0:T(128)S(1)} %add_convert_fusion, f32[64]{0:T(128)S(1)} %iota_multiply_fusion), kind=kOutput, calls=%fused_computation.10 | convolution fusion | flops 99288064 | bytes 9913344 | tf_op jit(solution)/shard_map/tf,frk->trk/dot_general | solution.py:47
  336.6 2.6 fusion.61
  339.2 5.2 %add_multiply_fusion = f32[64,80,192]{2,0,1:T(8,128)S(1)} fusion(f32[64,80,192]{2,0,1:T(8,128)S(1)} %fusion.32, s32[80,192]{1,0:T(8,128)S(1)} %copy.111, f32[8,80,2,192]{3,0,1,2:T(8,128)S(1)} %get-tuple-element.48, f32[8]{0:T(128)S(1)} %add_convert_fusion, f32[64]{0:T(128)S(1)} %iota_multiply_fusion), kind=kOutput, calls=%fused_computation.9 | convolution fusion | flops 99288064 | bytes 9913344 | tf_op jit(solution)/shard_map/tf,frk->trk/dot_general | solution.py:47
  344.5 2.7 fusion.17
  347.1 2.8 fusion.58
  350.0 2.7 fusion.15
  354.2 3.7 all-to-all-start.2
  358.5 2.2 copy.147
  360.7 14.4 %all-to-all-done.2 = f32[8,80,2,192]{3,1,2,0:T(8,128)S(1)} async-done(((f32[8,80,2,192]{3,1,2,0:T(8,128)}), f32[8,80,2,192]{3,1,2,0:T(8,128)S(1)}, u32[]{:S(2)}, u32[]{:S(2)}) %all-to-all-start.2) | async-done | bytes 983072 | tf_op jit(solution)/shard_map/all_to_all | solution.py:93
  378.7 28.6 %all-gather.6.cloned.1.call-done = bf16[2,2560,2,192]{3,2,0,1:T(2,128)(2,1)} async-done(((bf16[2,320,2,192]{3,2,0,1:T(2,128)(2,1)}), bf16[2,2560,2,192]{3,2,0,1:T(2,128)(2,1)}) %all-gather.6.cloned.1.call-update) | async-done | bytes 3932176 | tf_op jit(solution)/shard_map/all_gather | solution.py:109
  407.3 10.1 %fusion.9 = f32[2,2,320,2,192]{2,4,1,3,0:T(8,128)S(1)} fusion(bf16[2,2,320,2560]{3,2,1,0:T(8,128)(2,1)} %param.6, bf16[2,2560,2,192,1]{3,2,0,1,4:T(2,128)(2,1)} %bitcast.174), kind=kOutput, calls=%fused_computation.26 | convolution fusion | flops 2516582400 | bytes 12451840 | tf_op jit(solution)/shard_map/fpnm,fmqk->fpnqk/dot_general | solution.py:96
  419.7 38.6 %psum.30 = f32[]{:T(128)} all-reduce(f32[]{:T(128)} %multiply_reduce_fusion.1), channel_id=1, replica_groups=mesh['freq'=4,'rcv'=8] {'freq','rcv'}, use_global_device_ids=true, to_apply=%region_5.0 | all-reduce | flops 1 | bytes 8 | tf_op jit(solution)/shard_map/psum | solution.py:111
  458.9 2.5 multiply_add_fusion
  463.4 21.5 %psum.31 = f32[2,2,192]{2,0,1:T(2,128)S(1)} all-reduce(f32[2,2,192]{2,0,1:T(2,128)S(1)} %pad_maximum_fusion.5), channel_id=1, replica_groups=mesh['freq'=4,'rcv'=8] {'rcv'}, use_global_device_ids=true, to_apply=%region_8.0 | all-reduce | flops 768 | bytes 6144 | tf_op jit(solution)/shard_map/psum | solution.py:125
  (112 shorter events, 49.3 us)
Async XLA Ops:
  7.2 5.3 %copy-start = (s32[320,192]{0,1:T(8,128)S(1)}, s32[320,192]{0,1:T(8,128)}, u32[]{:S(2)}) copy-start(s32[320,192]{0,1:T(8,128)} %param.7) | copy-start | bytes 737284
  7.2 92.2 %all-gather.4.cloned.1.call-start = ((), (), s32[]{:S(2)}) async-start(), calls=%async_computation.3 | async-start | bytes 5898240 | tf_op jit(solution)/shard_map/all_gather | solution.py:100
  8.6 1.9 copy-start.6
  10.4 175.8 %all-gather.8.cloned.1.call-start = ((), (), s32[]{:S(2)}) async-start(), calls=%async_computation.5 | async-start | bytes 5898240 | tf_op jit(solution)/shard_map/all_gather | solution.py:113
  10.6 2.6 copy-start.12
  107.6 3.3 copy-start.14
  107.7 3.4 copy-start.13
  109.1 5.0 %collective-permute-start = (f32[2,80,2,192]{1,3,0,2:T(8,128)}, f32[2,80,2,192]{1,3,0,2:T(8,128)}, u32[]{:S(2)}, u32[]{:S(2)}) collective-permute-start(f32[2,80,2,192]{1,3,0,2:T(8,128)} %get-tuple-element.45), channel_id=1, source_target_pairs={{0,8},{8,0},{16,24},{24,16},{1,9},{9,1},{17,25},{25,17},{2,10},{10... | collective-permute-start | bytes 737288 | tf_op jit(solution)/shard_map/ppermute | solution.py:30
  109.1 12.1 %collective-permute-start.1 = (f32[2,80,2,192]{1,3,0,2:T(8,128)S(1)}, f32[2,80,2,192]{1,3,0,2:T(8,128)}, u32[]{:S(2)}, u32[]{:S(2)}) collective-permute-start(f32[2,80,2,192]{1,3,0,2:T(8,128)S(1)} %get-tuple-element.46), channel_id=1, source_target_pairs={{0,16},{8,24},{16,0},{24,8},{1,17},{9,25},{17,1},{25,9},{2,18},{10... | collective-permute-start | bytes 737288 | tf_op jit(solution)/shard_map/ppermute | solution.py:30
  110.5 18.1 %collective-permute-start.2 = (f32[2,80,2,192]{1,3,0,2:T(8,128)}, f32[2,80,2,192]{1,3,0,2:T(8,128)}, u32[]{:S(2)}, u32[]{:S(2)}) collective-permute-start(f32[2,80,2,192]{1,3,0,2:T(8,128)} %get-tuple-element.43), channel_id=1, source_target_pairs={{0,24},{8,16},{16,8},{24,0},{1,25},{9,17},{17,9},{25,1},{2,26},{10... | collective-permute-start | bytes 737288 | tf_op jit(solution)/shard_map/ppermute | solution.py:30
  130.6 1.0 copy-start.11
  162.9 32.4 %all-to-all-start = ((f32[8,80,2,192]{3,1,2,0:T(8,128)}), f32[8,80,2,192]{3,1,2,0:T(8,128)S(1)}, u32[]{:S(2)}, u32[]{:S(2)}) async-start(f32[8,80,2,192]{3,1,2,0:T(8,128)} %copy.120), calls=%async_computation | async-start | bytes 2621440 | tf_op jit(solution)/shard_map/all_to_all | solution.py:93
  166.4 240.8 %all-gather.6.cloned.1.call-start = ((), (), s32[]{:S(2)}) async-start(), calls=%async_computation.4 | async-start | bytes 5898240 | tf_op jit(solution)/shard_map/all_gather | solution.py:109
  242.0 8.5 %collective-permute-start.6 = (f32[2,80,2,192]{1,3,0,2:T(8,128)}, f32[2,80,2,192]{1,3,0,2:T(8,128)S(1)}, u32[]{:S(2)}, u32[]{:S(2)}) collective-permute-start(f32[2,80,2,192]{1,3,0,2:T(8,128)} %get-tuple-element.39), channel_id=1, source_target_pairs={{0,8},{8,0},{16,24},{24,16},{1,9},{9,1},{17,25},{25,17},{2,10},{10... | collective-permute-start | bytes 737288 | tf_op jit(solution)/shard_map/ppermute | solution.py:30
  242.1 12.6 %collective-permute-start.7 = (f32[2,80,2,192]{1,3,0,2:T(8,128)}, f32[2,80,2,192]{1,3,0,2:T(8,128)}, u32[]{:S(2)}, u32[]{:S(2)}) collective-permute-start(f32[2,80,2,192]{1,3,0,2:T(8,128)} %get-tuple-element.38), channel_id=1, source_target_pairs={{0,16},{8,24},{16,0},{24,8},{1,17},{9,25},{17,1},{25,9},{2,18},{10... | collective-permute-start | bytes 737288 | tf_op jit(solution)/shard_map/ppermute | solution.py:30
  244.4 18.3 %collective-permute-start.8 = (f32[2,80,2,192]{1,3,0,2:T(8,128)}, f32[2,80,2,192]{1,3,0,2:T(8,128)}, u32[]{:S(2)}, u32[]{:S(2)}) collective-permute-start(f32[2,80,2,192]{1,3,0,2:T(8,128)} %get-tuple-element.37), channel_id=1, source_target_pairs={{0,24},{8,16},{16,8},{24,0},{1,25},{9,17},{17,9},{25,1},{2,26},{10... | collective-permute-start | bytes 737288 | tf_op jit(solution)/shard_map/ppermute | solution.py:30
  244.6 1.3 copy-start.4
  246.6 1.4 copy-start.2
  248.1 15.8 %collective-permute-start.3 = (f32[2,80,2,192]{3,0,1,2:T(2,128)}, f32[2,80,2,192]{3,0,1,2:T(2,128)}, u32[]{:S(2)}, u32[]{:S(2)}) collective-permute-start(f32[2,80,2,192]{3,0,1,2:T(2,128)} %get-tuple-element.35), channel_id=1, source_target_pairs={{0,8},{8,0},{16,24},{24,16},{1,9},{9,1},{17,25},{25,17},{2,10},{10... | collective-permute-start | bytes 737288 | tf_op jit(solution)/shard_map/ppermute | solution.py:30
  248.2 21.9 %collective-permute-start.4 = (f32[2,80,2,192]{3,0,1,2:T(2,128)}, f32[2,80,2,192]{3,0,1,2:T(2,128)}, u32[]{:S(2)}, u32[]{:S(2)}) collective-permute-start(f32[2,80,2,192]{3,0,1,2:T(2,128)} %get-tuple-element.34), channel_id=1, source_target_pairs={{0,16},{8,24},{16,0},{24,8},{1,17},{9,25},{17,1},{25,9},{2,18},{10... | collective-permute-start | bytes 737288 | tf_op jit(solution)/shard_map/ppermute | solution.py:30
  250.5 0.7 copy-start.15
  251.3 25.4 %collective-permute-start.5 = (f32[2,80,2,192]{3,0,1,2:T(2,128)}, f32[2,80,2,192]{3,0,1,2:T(2,128)}, u32[]{:S(2)}, u32[]{:S(2)}) collective-permute-start(f32[2,80,2,192]{3,0,1,2:T(2,128)} %get-tuple-element.33), channel_id=1, source_target_pairs={{0,24},{8,16},{16,8},{24,0},{1,25},{9,17},{17,9},{25,1},{2,26},{10... | collective-permute-start | bytes 737288 | tf_op jit(solution)/shard_map/ppermute | solution.py:30
  354.2 4.3 copy-start.3
  354.2 20.9 %all-to-all-start.2 = ((f32[8,80,2,192]{3,1,2,0:T(8,128)}), f32[8,80,2,192]{3,1,2,0:T(8,128)S(1)}, u32[]{:S(2)}, u32[]{:S(2)}) async-start(f32[8,80,2,192]{3,1,2,0:T(8,128)} %copy.142), calls=%async_computation.2 | async-start | bytes 2621440 | tf_op jit(solution)/shard_map/all_to_all | solution.py:93
  417.5 1.1 copy-start.8
  417.6 41.3 %copy-start.5 = (f32[2,320,2,192]{1,3,2,0:T(8,128)S(1)}, f32[2,320,2,192]{1,3,2,0:T(8,128)}, u32[]{:S(2)}) copy-start(f32[2,320,2,192]{1,3,2,0:T(8,128)} %param.10) | copy-start | bytes 2949124
  461.4 1.3 copy-start.9
  461.4 1.7 copy-start.10
  463.1 22.4 %copy-start.7 = (f32[2,320,2,192]{1,3,0,2:T(8,128)S(1)}, f32[2,320,2,192]{1,3,0,2:T(8,128)}, u32[]{:S(2)}) copy-start(f32[2,320,2,192]{1,3,0,2:T(8,128)} %get-tuple-element.41) | copy-start | bytes 2949124
  463.1 23.5 %copy-start.1 = (s32[320,192]{0,1:T(8,128)S(1)}, s32[320,192]{0,1:T(8,128)}, u32[]{:S(2)}) copy-start(s32[320,192]{0,1:T(8,128)} %param.7) | copy-start | bytes 737284
Sparse Core Ops, SparseCore 0:
  10.7 88.5 all-gather.3
  102.1 84.0 all-gather.7
  322.4 84.8 all-gather.5
